TPU v7x, 32 devices: a whole 2x2x4 slice. The times are simulated.
32 devices in a mesh: row: 4 (over y, x), col: 8 (over z, core).
Axes of the slice: x: 2, y: 2, z: 4, core: 2. Of those that a mesh axis runs over, the one named last changes fastest.
Arguments:
- matrix: float32 [256, 40960], P('row', 'col'), as said below
- pivots: int32 [256], replicated, may hold values from 0 to 255, as said below
- check_weights: float32 [2, 256], P(None, 'row'), may hold values from -0.375 to 0.375
- checksum: float32 [2, 40960], P(None, 'col'), may hold values from -6 to 6
- coefficients: float32 [4, 8], P('row', 'col'), may hold values from 0.125 to 0.5
- checkpoints: int32 [4, 2], P('row'), may hold values from 0 to 3, as said below
Outputs:
- updated: float32 [256, 40960], P('row', 'col')
- new_checksum: float32 [2, 40960], P(None, 'col')
- parity: float32 [256, 40960], P('row', 'col')
Inputs may be any that keep to these rules, and one draw needn't show every extreme that they name: `pivots`: 256 distinct row numbers. `checkpoints`: row index 0 keeps both codes on member 4 - 1, row index 1 on member 0. `matrix`: the first 256 columns are the panel's multipliers, of size about 256 ** -0.5.
All inputs are finite; a program needn't handle non-finite values.
Results may differ from a plain program's by a relative error of at most 0.000098.
Values sent between devices are 32-bit elements; how exact they have to be, the bound alone decides.
No kernel may reach another device: no remote copies, remote signals or barrier semaphores. Data moves between devices by JAX's collectives and lax.ppermute only.
A program may use at most 64 MiB of HBM per device.

v0:
```python
import jax
import jax.numpy as jnp
from jax import lax
from jax.sharding import PartitionSpec as P


def spread(value, axis, source):
    kept = jnp.where(lax.axis_index(axis) == source, value, 0).astype(value.dtype)
    return lax.psum(kept, axis)


def from_partner(block, axis, bit):
    count = lax.axis_size(axis)
    route = []
    for low in range(count):
        high = low | 1 << bit
        if high != low and high < count:
            route += [(low, high), (high, low)]
    return lax.ppermute(block, axis, route)


def per_device(matrix, pivots, check_weights, checksum, coefficients, checkpoints):
    rows_local = matrix.shape[0]
    cols_local = matrix.shape[1]
    width = pivots.shape[0]
    checks = check_weights.shape[0]
    row_index = lax.axis_index("row")
    col_index = lax.axis_index("col")
    lower = spread(matrix[:, :width], "col", 0)
    local_rows = pivots - row_index * rows_local
    selector = (local_rows[:, None] == jnp.arange(rows_local, dtype=jnp.int32)[None, :]).astype(
        jnp.float32
    )
    picked = jnp.dot(
        selector, matrix, preferred_element_type=jnp.float32, precision=lax.Precision.HIGHEST
    )
    weighted_part = jnp.dot(
        check_weights, lower, preferred_element_type=jnp.float32, precision=lax.Precision.HIGHEST
    )
    padded_part = jnp.pad(weighted_part, ((0, 0), (0, cols_local - width)))
    stacked = lax.psum(jnp.concatenate([picked, padded_part], axis=0), "row")
    picked = stacked[:width]
    weighted_lower = stacked[width : width + checks, :width]
    column_ids = col_index * cols_local + jnp.arange(cols_local, dtype=jnp.int32)
    upper = jnp.where(column_ids[None, :] >= width, picked, jnp.float32(0.0))
    updated = matrix - jnp.dot(
        lower, upper, preferred_element_type=jnp.float32, precision=lax.Precision.HIGHEST
    )
    new_checksum = checksum - jnp.dot(
        weighted_lower, upper, preferred_element_type=jnp.float32, precision=lax.Precision.HIGHEST
    )
    own = matrix * coefficients[0, 0]
    position = col_index // 2
    group_id = col_index % 2
    keeper = jnp.where(group_id == 0, checkpoints[0, 0], checkpoints[0, 1])
    levels = lax.axis_size("col").bit_length() - 1
    piece = own
    for level in range(1, levels):
        half = piece.shape[1] // 2
        bit_value = col_index // 2**level % 2
        first_half = piece[:, :half]
        second_half = piece[:, half:]
        outgoing = jnp.where(bit_value == 0, second_half, first_half)
        kept = jnp.where(bit_value == 0, first_half, second_half)
        piece = kept + from_partner(outgoing, "col", level)
    for level in range(levels - 1, 0, -1):
        bit_value = col_index // 2**level % 2
        partner = from_partner(piece, "col", level)
        piece = jnp.where(
            bit_value == 0,
            jnp.concatenate([piece, partner], axis=1),
            jnp.concatenate([partner, piece], axis=1),
        )
    parity = jnp.where(position == keeper, piece, jnp.float32(0.0))
    return (updated, new_checksum, parity)


def solution(mesh):
    in_specs = (
        P("row", "col"),
        P(),
        P(None, "row"),
        P(None, "col"),
        P("row", "col"),
        P("row", None),
    )
    out_specs = (P("row", "col"), P(None, "col"), P("row", "col"))
    return jax.shard_map(
        per_device, mesh=mesh, in_specs=in_specs, out_specs=out_specs, check_vma=False
    )
```

profile of v0, /device:TPU:0, one launch (start us, length us, event | category | flops | bytes accessed | tf_op | source)
XLA Modules:
  0.0 215.2 jit_solution(14134000331034751280)
XLA Ops:
  7.2 0.0 copy-start
  7.2 0.0 all-reduce.4.cloned.1.call-start
  7.2 1.5 slice_select_fusion.5
  8.7 0.0 all-reduce.4.cloned.1.call-update
  8.7 0.0 all-reduce.6.cloned.1.call-start
  9.4 0.0 copy-start.6
  9.4 0.0 copy-start.2
  9.5 1.5 broadcast_multiply_fusion
  11.0 0.0 copy-done.6
  11.0 0.2 copy-done.2
  11.2 4.6 %fusion.5 = f32[256,5120]{1,0:T(8,128)} fusion(f32[64,5120]{1,0:T(8,128)S(1)} %copy-done.2, s32[256]{0:T(256)S(1)} %broadcast_subtract_fusion), kind=kOutput, calls=%fused_computation.19 | convolution fusion | flops 1006649344 | bytes 6554624 | tf_op jit(solution)/shard_map/dot_general | solution.py:34
  15.7 52.6 %all-reduce.4.cloned.1.call-done = f32[64,256]{1,0:T(8,128)} async-done(((f32[64,256]{1,0:T(8,128)}), f32[64,256]{1,0:T(8,128)}) %all-reduce.4.cloned.1.call-update) | async-done | bytes 65552 | tf_op jit(solution)/shard_map/psum | solution.py:9
  68.3 0.0 copy-done
  68.3 1.0 convolution_bitcast_fusion
  69.3 5.6 %select_maximum_fusion = f32[258,5120]{1,0:T(8,128)} fusion(f32[2,256]{1,0:T(2,128)S(1)} %convolution_bitcast_fusion, f32[256,5120]{1,0:T(8,128)} %fusion.5), kind=kLoop, calls=%fused_computation.2 | loop fusion | flops 3962880 | bytes 10528768 | tf_op jit(solution)/shard_map/concatenate | solution.py:41
  74.9 0.0 all-reduce.6.cloned.1.call-update
  74.9 0.1 slice_select_fusion.3
  75.0 0.6 collective-permute-start
  75.6 14.3 %collective-permute-done = f32[64,2560]{1,0:T(8,128)} collective-permute-done((f32[64,2560]{1,0:T(8,128)S(1)}, f32[64,2560]{1,0:T(8,128)}, u32[]{:S(2)}, u32[]{:S(2)}) %collective-permute-start) | collective-permute-done | bytes 655392 | tf_op jit(solution)/shard_map/ppermute | solution.py:19
  89.9 1.4 select_add_fusion
  91.3 0.0 copy-start.5
  91.3 1.2 collective-permute-start.1
  92.5 13.6 %collective-permute-done.1 = f32[64,1280]{1,0:T(8,128)S(1)} collective-permute-done((f32[64,1280]{1,0:T(8,128)S(1)}, f32[64,1280]{1,0:T(8,128)S(1)}, u32[]{:S(2)}, u32[]{:S(2)}) %collective-permute-start.1) | collective-permute-done | bytes 327712 | tf_op jit(solution)/shard_map/ppermute | solution.py:19
  106.2 0.1 collective-permute-start.2
  106.2 16.8 %collective-permute-done.2 = f32[64,1280]{1,0:T(8,128)S(1)} collective-permute-done((f32[64,1280]{1,0:T(8,128)S(1)}, f32[64,1280]{1,0:T(8,128)S(1)}, u32[]{:S(2)}, u32[]{:S(2)}) %collective-permute-start.2) | collective-permute-done | bytes 327712 | tf_op jit(solution)/shard_map/ppermute | solution.py:19
  123.1 0.1 collective-permute-start.3
  123.2 0.0 copy-done.5
  123.2 0.6 fusion.10
  125.1 0.0 copy-start.3
  125.1 14.3 %collective-permute-done.3 = f32[64,2560]{1,0:T(8,128)S(1)} collective-permute-done((f32[64,2560]{1,0:T(8,128)S(1)}, f32[64,2560]{1,0:T(8,128)S(1)}, u32[]{:S(2)}, u32[]{:S(2)}) %collective-permute-start.3) | collective-permute-done | bytes 655392 | tf_op jit(solution)/shard_map/ppermute | solution.py:19
  139.4 1.2 fusion.4
  140.6 0.0 copy-start.4
  140.6 57.4 %all-reduce.6.cloned.1.call-done = f32[258,5120]{1,0:T(8,128)} async-done(((f32[258,5120]{1,0:T(8,128)}), f32[258,5120]{1,0:T(8,128)}) %all-reduce.6.cloned.1.call-update) | async-done | bytes 5283856 | tf_op jit(solution)/shard_map/psum | solution.py:41
  197.9 0.0 copy-done.3
  197.9 0.0 copy-start.1
  197.9 7.1 %convolution_subtract_fusion = f32[64,5120]{1,0:T(8,128)} fusion(f32[64,5120]{1,0:T(8,128)S(1)} %copy-done.2, f32[64,256]{1,0:T(8,128)S(1)} %copy-done.3, f32[258,5120]{1,0:T(8,128)} %all-reduce.6.cloned.1.call-done, pred[5120]{0:T(1024)(128)(4,1)S(1)} %add_compare_fusion), kind=kOutput, calls=%fused_computation | convolution fusion | flops 1008271360 | bytes 7934976 | tf_op jit(solution)/shard_map/dot_general | solution.py:46
  205.0 0.0 copy-done.4
  205.0 0.0 copy-done.1
  205.0 3.3 %convolution_subtract_fusion.1 = f32[2,5120]{1,0:T(2,128)} fusion(f32[2,5120]{1,0:T(2,128)S(1)} %copy-done.4, f32[258,5120]{1,0:T(8,128)S(1)} %copy-done.1, pred[5120]{0:T(1024)(128)(4,1)S(1)} %add_compare_fusion), kind=kOutput, calls=%fused_computation.1 | convolution fusion | flops 32778240 | bytes 5331968 | tf_op jit(solution)/shard_map/dot_general | solution.py:49
  (5 shorter events, 0.1 us)
Async XLA Ops:
  7.2 61.2 %copy-start = (f32[2,64]{1,0:T(2,128)S(1)}, f32[2,64]{1,0:T(2,128)}, u32[]{:S(2)}) copy-start(f32[2,64]{1,0:T(2,128)} %param.8) | copy-start | bytes 1540
  7.2 61.1 %all-reduce.4.cloned.1.call-start = ((), (), s32[]{:S(2)}) async-start(), calls=%async_computation | async-start | bytes 131072 | tf_op jit(solution)/shard_map/psum | solution.py:9
  8.7 189.2 %all-reduce.6.cloned.1.call-start = ((), (), s32[]{:S(2)}) async-start(), calls=%async_computation.1 | async-start | bytes 10813440 | tf_op jit(solution)/shard_map/psum | solution.py:41
  9.4 1.6 copy-start.6
  9.4 1.7 copy-start.2
  75.0 14.9 %collective-permute-start = (f32[64,2560]{1,0:T(8,128)S(1)}, f32[64,2560]{1,0:T(8,128)}, u32[]{:S(2)}, u32[]{:S(2)}) collective-permute-start(f32[64,2560]{1,0:T(8,128)S(1)} %slice_select_fusion.3), channel_id=1, source_target_pairs={{0,2},{2,0},{1,3},{3,1},{4,6},{6,4},{5,7},{7,5},{8,10},{10,8},{9,1... | collective-permute-start | bytes 1966088 | tf_op jit(solution)/shard_map/ppermute | solution.py:19
  91.3 31.9 %copy-start.5 = (s32[1,2]{1,0:T(1,128)S(1)}, s32[1,2]{1,0:T(1,128)}, u32[]{:S(2)}) copy-start(s32[1,2]{1,0:T(1,128)} %param.11) | copy-start | bytes 28
  91.3 14.8 %collective-permute-start.1 = (f32[64,1280]{1,0:T(8,128)S(1)}, f32[64,1280]{1,0:T(8,128)S(1)}, u32[]{:S(2)}, u32[]{:S(2)}) collective-permute-start(f32[64,1280]{1,0:T(8,128)S(1)} %slice_select_fusion.4), channel_id=1, source_target_pairs={{0,4},{4,0},{1,5},{5,1},{2,6},{6,2},{3,7},{7,3},{8,12},{12,8},{9,1... | collective-permute-start | bytes 983048 | tf_op jit(solution)/shard_map/ppermute | solution.py:19
  106.2 16.9 %collective-permute-start.2 = (f32[64,1280]{1,0:T(8,128)S(1)}, f32[64,1280]{1,0:T(8,128)S(1)}, u32[]{:S(2)}, u32[]{:S(2)}) collective-permute-start(f32[64,1280]{1,0:T(8,128)S(1)} %select_add_fusion.1), channel_id=1, source_target_pairs={{0,4},{4,0},{1,5},{5,1},{2,6},{6,2},{3,7},{7,3},{8,12},{12,8},{9,1... | collective-permute-start | bytes 983048 | tf_op jit(solution)/shard_map/ppermute | solution.py:19
  123.1 16.3 %collective-permute-start.3 = (f32[64,2560]{1,0:T(8,128)S(1)}, f32[64,2560]{1,0:T(8,128)S(1)}, u32[]{:S(2)}, u32[]{:S(2)}) collective-permute-start(f32[64,2560]{1,0:T(8,128)S(1)} %maximum_select_fusion.1), channel_id=1, source_target_pairs={{0,2},{2,0},{1,3},{3,1},{4,6},{6,4},{5,7},{7,5},{8,10},{10,8},{9,1... | collective-permute-start | bytes 1966088 | tf_op jit(solution)/shard_map/ppermute | solution.py:19
  125.1 72.8 %copy-start.3 = (f32[64,256]{1,0:T(8,128)S(1)}, f32[64,256]{1,0:T(8,128)}, u32[]{:S(2)}) copy-start(f32[64,256]{1,0:T(8,128)} %all-reduce.4.cloned.1.call-done) | copy-start | bytes 196612
  140.6 64.4 %copy-start.4 = (f32[2,5120]{1,0:T(2,128)S(1)}, f32[2,5120]{1,0:T(2,128)}, u32[]{:S(2)}) copy-start(f32[2,5120]{1,0:T(2,128)} %param.9) | copy-start | bytes 122884
  197.9 7.1 %copy-start.1 = (f32[258,5120]{1,0:T(8,128)S(1)}, f32[258,5120]{1,0:T(8,128)}, u32[]{:S(2)}) copy-start(f32[258,5120]{1,0:T(8,128)} %all-reduce.6.cloned.1.call-done) | copy-start | bytes 15851524
Sparse Core Ops, SparseCore 0:
  10.9 57.4 all-reduce.3
  75.0 122.8 all-reduce.5
where the time goes:
time: 216 us; the launch traced here: 215 us
  waiting for transfers between devices  169 us (78%)
  between operations  16.1 us (7%)
  matrix products  15.9 us (7%)
  other arithmetic  11.3 us (5%)
    ppermute x4, waiting for transfers between devices, from_partner(): return lax.ppermute(block, axis, route)  59 us
    psum x1, waiting for transfers between devices, per_device(): stacked = lax.psum(jnp.concatenate([picked, padded_part], axis=0), 'row')  57.4 us
    psum x1, waiting for transfers between devices, spread(): return lax.psum(kept, axis)  52.6 us
    dot_general x1, matrix products, per_device(): jnp.dot(lower, upper, preferred_element_type=jnp.float32, precision=lax.P...  7.08 us
    concatenate x1, other arithmetic, per_device(): stacked = lax.psum(jnp.concatenate([picked, padded_part], axis=0), 'row')  5.58 us
    dot_general x1, matrix products, per_device(): jnp.dot(selector, matrix, preferred_element_type=jnp.float32, precision=l...  4.57 us
  transfers between devices with their start and end apart: 6, of which 6 were waited for; matrix products, arithmetic and copies ran while one was open for 4% of the time, Pallas kernels for 0%

commit v1 on v0

--- a/solution.py
+++ b/solution.py
@@ -38,7 +38,7 @@
         check_weights, lower, preferred_element_type=jnp.float32, precision=lax.Precision.HIGHEST
     )
     padded_part = jnp.pad(weighted_part, ((0, 0), (0, cols_local - width)))
-    stacked = lax.psum(jnp.concatenate([picked, padded_part], axis=0), "row")
+    stacked = jnp.sum(lax.all_gather(jnp.concatenate([picked, padded_part], axis=0), "row"), axis=0)
     picked = stacked[:width]
     weighted_lower = stacked[width : width + checks, :width]
     column_ids = col_index * cols_local + jnp.arange(cols_local, dtype=jnp.int32)

time: 216 us -> 304 us (1.41)
  waiting for transfers between devices: 169 us -> 242 us
  other arithmetic: 11.3 us -> 22.1 us
  matrix products: 15.9 us -> 19.6 us
    all_gather x0 -> x1, waiting for transfers between devices: none -> 130 us  [per_device(): lax.all_gather(jnp.concatenate([picked, padded_part], axis=0), 'row')]
    psum x1 -> x0, waiting for transfers between devices: 57.4 us -> none  [per_device(): stacked = lax.psum(jnp.concatenate([picked, padded_part], axis=0), 'row')]
    reduce_sum x0 -> x1, other arithmetic: none -> 11.4 us  [per_device(): jnp.sum(lax.all_gather(jnp.concatenate([picked, padded_part], axis=0), 'r...]
    concatenate x1 -> x0, other arithmetic: 5.58 us -> none  [per_device(): stacked = lax.psum(jnp.concatenate([picked, padded_part], axis=0), 'row')]
    unnamed x0 -> x1, other arithmetic: none -> 5.55 us
  transfers between devices with their start and end apart: 6 -> 6, of which waited for: 6 -> 6; matrix products, arithmetic and copies ran while one was open for 4% -> 3% of each run, Pallas kernels for 0% -> 0%
where the time goes in v1:
time: 304 us
  waiting for transfers between devices  242 us (80%)
  other arithmetic  22.1 us (7%)
  matrix products  19.6 us (6%)
  between operations  16.2 us (5%)
    all_gather x1, waiting for transfers between devices, per_device(): lax.all_gather(jnp.concatenate([picked, padded_part], axis=0), 'row')  130 us
    ppermute x4, waiting for transfers between devices, from_partner(): return lax.ppermute(block, axis, route)  59 us
    psum x1, waiting for transfers between devices, spread(): return lax.psum(kept, axis)  53 us
    reduce_sum x1, other arithmetic, per_device(): jnp.sum(lax.all_gather(jnp.concatenate([picked, padded_part], axis=0), 'r...  11.4 us
    dot_general x1, matrix products, per_device(): jnp.dot(lower, upper, preferred_element_type=jnp.float32, precision=lax.P...  6.93 us
  transfers between devices with their start and end apart: 6, of which 6 were waited for; matrix products, arithmetic and copies ran while one was open for 3% of the time, Pallas kernels for 0%

profile of v1, /device:TPU:0, one launch (start us, length us, event | category | flops | bytes accessed | tf_op | source)
XLA Modules:
  0.0 303.6 jit_solution(14740598045898511997)
XLA Ops:
  7.2 0.0 copy-start
  7.2 0.0 all-reduce.3.cloned.1.call-start
  7.2 1.5 slice_select_fusion.5
  8.7 0.0 all-reduce.3.cloned.1.call-update
  8.7 0.0 all-gather.4.cloned.1.call-start
  8.8 0.7 broadcast_subtract_fusion
  9.5 5.9 %fusion.6 = f32[256,5120]{1,0:T(8,128)} fusion(f32[64,5120]{1,0:T(8,128)} %param.6, s32[256]{0:T(256)S(1)} %broadcast_subtract_fusion), kind=kOutput, calls=%fused_computation.20 | convolution fusion | flops 1006649344 | bytes 6554624 | tf_op jit(solution)/shard_map/dot_general | solution.py:34
  15.3 53.0 %all-reduce.3.cloned.1.call-done = f32[64,256]{1,0:T(8,128)} async-done(((f32[64,256]{1,0:T(8,128)}), f32[64,256]{1,0:T(8,128)}) %all-reduce.3.cloned.1.call-update) | async-done | bytes 65552 | tf_op jit(solution)/shard_map/psum | solution.py:9
  68.3 0.0 copy-done
  68.3 1.0 convolution_bitcast_fusion
  69.3 5.6 %fusion = f32[1,258,5120]{2,1,0:T(8,128)} fusion(f32[2,256]{1,0:T(2,128)S(1)} %convolution_bitcast_fusion, f32[256,5120]{1,0:T(8,128)} %fusion.6), kind=kLoop, calls=%fused_computation.3 | loop fusion | flops 3962880 | bytes 10528768
  74.9 0.0 copy-start.1
  74.9 0.0 all-gather.4.cloned.1.call-update
  75.7 0.5 copy-done.1
  76.2 0.1 broadcast_multiply_fusion
  76.3 0.1 slice_select_fusion.3
  76.4 0.6 collective-permute-start
  77.0 14.3 %collective-permute-done = f32[64,2560]{1,0:T(8,128)} collective-permute-done((f32[64,2560]{1,0:T(8,128)S(1)}, f32[64,2560]{1,0:T(8,128)}, u32[]{:S(2)}, u32[]{:S(2)}) %collective-permute-start) | collective-permute-done | bytes 655392 | tf_op jit(solution)/shard_map/ppermute | solution.py:19
  91.3 1.4 select_add_fusion
  92.8 0.0 copy-start.4
  92.8 1.3 collective-permute-start.1
  94.1 13.4 %collective-permute-done.1 = f32[64,1280]{1,0:T(8,128)S(1)} collective-permute-done((f32[64,1280]{1,0:T(8,128)S(1)}, f32[64,1280]{1,0:T(8,128)S(1)}, u32[]{:S(2)}, u32[]{:S(2)}) %collective-permute-start.1) | collective-permute-done | bytes 327712 | tf_op jit(solution)/shard_map/ppermute | solution.py:19
  107.5 0.1 select_add_fusion.1
  107.6 0.1 collective-permute-start.2
  107.7 16.8 %collective-permute-done.2 = f32[64,1280]{1,0:T(8,128)S(1)} collective-permute-done((f32[64,1280]{1,0:T(8,128)S(1)}, f32[64,1280]{1,0:T(8,128)S(1)}, u32[]{:S(2)}, u32[]{:S(2)}) %collective-permute-start.2) | collective-permute-done | bytes 327712 | tf_op jit(solution)/shard_map/ppermute | solution.py:19
  124.6 0.1 collective-permute-start.3
  124.7 0.0 copy-done.4
  124.7 0.6 fusion.11
  126.6 14.5 %collective-permute-done.3 = f32[64,2560]{1,0:T(8,128)S(1)} collective-permute-done((f32[64,2560]{1,0:T(8,128)S(1)}, f32[64,2560]{1,0:T(8,128)S(1)}, u32[]{:S(2)}, u32[]{:S(2)}) %collective-permute-start.3) | collective-permute-done | bytes 655392 | tf_op jit(solution)/shard_map/ppermute | solution.py:19
  141.0 1.2 fusion.5
  142.2 0.0 copy-start.3
  142.2 130.3 %all-gather.4.cloned.1.call-done = f32[4,258,5120]{2,1,0:T(8,128)} async-done(((f32[1,258,5120]{2,1,0:T(8,128)}), f32[4,258,5120]{2,1,0:T(8,128)}) %all-gather.4.cloned.1.call-update) | async-done | bytes 21135376 | tf_op jit(solution)/shard_map/all_gather | solution.py:41
  272.6 11.4 %reduce_sum.9 = f32[258,5120]{1,0:T(8,128)} reduce(f32[4,258,5120]{2,1,0:T(8,128)} %all-gather.4.cloned.1.call-done, f32[]{:T(128)} %constant.61.clone.1), dimensions={0}, to_apply=%region_1.2 | reduce | flops 3962880 | bytes 26419204 | tf_op jit(solution)/shard_map/reduce_sum | solution.py:41
  284.0 0.0 copy-done.3
  284.0 0.0 copy-start.2
  284.0 5.8 %convolution_subtract_fusion.1 = f32[2,5120]{1,0:T(2,128)} fusion(f32[2,5120]{1,0:T(2,128)S(1)} %copy-done.3, f32[258,5120]{1,0:T(8,128)} %reduce_sum.9, pred[5120]{0:T(1024)(128)(4,1)S(1)} %add_compare_fusion), kind=kOutput, calls=%fused_computation.1 | convolution fusion | flops 32778240 | bytes 5331968 | tf_op jit(solution)/shard_map/dot_general | solution.py:49
  289.8 0.0 copy-done.2
  289.8 6.9 %convolution_subtract_fusion = f32[64,5120]{1,0:T(8,128)} fusion(f32[64,5120]{1,0:T(8,128)S(1)} %copy-done.1, f32[64,256]{1,0:T(8,128)S(1)} %copy-done.2, f32[258,5120]{1,0:T(8,128)} %reduce_sum.9, pred[5120]{0:T(1024)(128)(4,1)S(1)} %add_compare_fusion), kind=kOutput, calls=%fused_computation | convolution fusion | flops 1008271360 | bytes 7934976 | tf_op jit(solution)/shard_map/dot_general | solution.py:46
  (3 shorter events, 0.1 us)
Async XLA Ops:
  7.2 61.2 %copy-start = (f32[2,64]{1,0:T(2,128)S(1)}, f32[2,64]{1,0:T(2,128)}, u32[]{:S(2)}) copy-start(f32[2,64]{1,0:T(2,128)} %param.8) | copy-start | bytes 1540
  7.2 61.1 %all-reduce.3.cloned.1.call-start = ((), (), s32[]{:S(2)}) async-start(), calls=%async_computation | async-start | bytes 131072 | tf_op jit(solution)/shard_map/psum | solution.py:9
  8.7 263.8 %all-gather.4.cloned.1.call-start = ((), (), s32[]{:S(2)}) async-start(), calls=%async_computation.1 | async-start | bytes 27033600 | tf_op jit(solution)/shard_map/all_gather | solution.py:41
  74.9 1.3 copy-start.1
  76.4 14.9 %collective-permute-start = (f32[64,2560]{1,0:T(8,128)S(1)}, f32[64,2560]{1,0:T(8,128)}, u32[]{:S(2)}, u32[]{:S(2)}) collective-permute-start(f32[64,2560]{1,0:T(8,128)S(1)} %slice_select_fusion.3), channel_id=1, source_target_pairs={{0,2},{2,0},{1,3},{3,1},{4,6},{6,4},{5,7},{7,5},{8,10},{10,8},{9,1... | collective-permute-start | bytes 1966088 | tf_op jit(solution)/shard_map/ppermute | solution.py:19
  92.8 31.9 %copy-start.4 = (s32[1,2]{1,0:T(1,128)S(1)}, s32[1,2]{1,0:T(1,128)}, u32[]{:S(2)}) copy-start(s32[1,2]{1,0:T(1,128)} %param.11) | copy-start | bytes 28
  92.8 14.8 %collective-permute-start.1 = (f32[64,1280]{1,0:T(8,128)S(1)}, f32[64,1280]{1,0:T(8,128)S(1)}, u32[]{:S(2)}, u32[]{:S(2)}) collective-permute-start(f32[64,1280]{1,0:T(8,128)S(1)} %slice_select_fusion.4), channel_id=1, source_target_pairs={{0,4},{4,0},{1,5},{5,1},{2,6},{6,2},{3,7},{7,3},{8,12},{12,8},{9,1... | collective-permute-start | bytes 983048 | tf_op jit(solution)/shard_map/ppermute | solution.py:19
  107.6 16.9 %collective-permute-start.2 = (f32[64,1280]{1,0:T(8,128)S(1)}, f32[64,1280]{1,0:T(8,128)S(1)}, u32[]{:S(2)}, u32[]{:S(2)}) collective-permute-start(f32[64,1280]{1,0:T(8,128)S(1)} %select_add_fusion.1), channel_id=1, source_target_pairs={{0,4},{4,0},{1,5},{5,1},{2,6},{6,2},{3,7},{7,3},{8,12},{12,8},{9,1... | collective-permute-start | bytes 983048 | tf_op jit(solution)/shard_map/ppermute | solution.py:19
  124.6 16.5 %collective-permute-start.3 = (f32[64,2560]{1,0:T(8,128)S(1)}, f32[64,2560]{1,0:T(8,128)S(1)}, u32[]{:S(2)}, u32[]{:S(2)}) collective-permute-start(f32[64,2560]{1,0:T(8,128)S(1)} %maximum_select_fusion.1), channel_id=1, source_target_pairs={{0,2},{2,0},{1,3},{3,1},{4,6},{6,4},{5,7},{7,5},{8,10},{10,8},{9,1... | collective-permute-start | bytes 1966088 | tf_op jit(solution)/shard_map/ppermute | solution.py:19
  142.2 141.8 %copy-start.3 = (f32[2,5120]{1,0:T(2,128)S(1)}, f32[2,5120]{1,0:T(2,128)}, u32[]{:S(2)}) copy-start(f32[2,5120]{1,0:T(2,128)} %param.9) | copy-start | bytes 122884
  284.0 5.8 %copy-start.2 = (f32[64,256]{1,0:T(8,128)S(1)}, f32[64,256]{1,0:T(8,128)}, u32[]{:S(2)}) copy-start(f32[64,256]{1,0:T(8,128)} %all-reduce.3.cloned.1.call-done) | copy-start | bytes 196612
Sparse Core Ops, SparseCore 0:
  10.9 57.4 all-reduce.2
  75.0 197.4 all-gather.3
